TPU v7x, 256 devices: a whole 4x4x8 slice. The times are simulated.
256 devices in a mesh: obs: 8 (over z_hi, core), gx: 8 (over y, z_lo), gy: 4 (over x).
Axes of the slice: x: 4, y: 4, z: 8 (z_hi: 4, z_lo: 2; z = z_hi * 2 + z_lo), core: 2. Of those that a mesh axis runs over, the one named last changes fastest.
Arguments:
- closing_costates: float32 [2, 32, 64, 64, 128], P(None, 'obs', 'gx', 'gy'), may hold values from -6.5 to 6.5
- saved_pore_load: float32 [3, 64, 64, 128], P(None, 'gx', 'gy', 'obs'), may hold values from -4 to 4
- saved_heat_field: float32 [3, 64, 64, 128], P(None, 'gx', 'gy', 'obs'), may hold values from -2.5 to -0.5
- saved_dilatation: float32 [3, 64, 64, 128], P(None, 'gx', 'gy', 'obs'), may hold values from -2.5 to -0.5
- saved_conductivity: float32 [3, 64, 64, 128], P(None, 'gx', 'gy', 'obs'), may hold values from 2.5 to 5
- data_residual: float32 [3, 32, 128], P(None, 'obs'), may hold values from -8 to 8
- borehole_flat_position: int32 [32], P('obs'), may hold values from 0 to 4095
- probe_multiplier: int32 [32], P('obs'), may hold values from 1 to 4
Outputs:
- adjoint_start: float32 [2, 32, 64, 64, 128], P(None, 'obs', 'gx', 'gy')
- gradient: float32 [64, 64, 128], P('gx', 'gy', 'obs')
All inputs are finite; a program needn't handle non-finite values.
Results may differ from a plain program's by a relative error of at most 0.0003.
Values sent between devices are 32-bit elements; how exact they have to be, the bound alone decides.
A program may use at most 64 MiB of HBM per device.

v0:
```python
import jax
import jax.numpy as jnp
from jax import lax
from jax.sharding import PartitionSpec as P

ITERS = 4
heat_diffusivity = 2.0


def padded_2(value, sides, width):
    for axis, dim in sides:
        count, length = (lax.axis_size(axis), value.shape[dim])
        up = [(i, (i + 1) % count) for i in range(count - 1)]
        down = [(j, i) for i, j in up]
        last = lax.slice_in_dim(value, length - width, length, axis=dim)
        initial = lax.slice_in_dim(value, 0, width, axis=dim)
        before = lax.ppermute(last, axis, up)
        after = lax.ppermute(initial, axis, down)
        value = jnp.concatenate([before, value, after], axis=dim)
    return value


def neighbour_sum(padded):
    centre = padded[..., 1:-1, 1:-1, :]
    widths = [(0, 0)] * (centre.ndim - 1) + [(1, 1)]
    deeper = jnp.pad(centre, widths)
    summed = padded[..., 2:, 1:-1, :] + padded[..., :-2, 1:-1, :]
    summed = summed + padded[..., 1:-1, 2:, :] + padded[..., 1:-1, :-2, :]
    return summed + deeper[..., 2:] + deeper[..., :-2]


def whole_faces(costate_vector):
    return padded_2(costate_vector, (("gx", 2), ("gy", 3)), 1)


def relax_group(costate_vector, rights, coeffs):
    perm_now, coupling, diag_p, heat_main_entry = coeffs
    padded = whole_faces(costate_vector)
    near = neighbour_sum(padded)
    new_p = (rights[0] + perm_now * near[0] + coupling * costate_vector[1]) / diag_p
    new_t = (rights[1] + heat_diffusivity * near[1] + coupling * new_p) / heat_main_entry
    return jnp.stack([new_p, new_t])


def local(
    closing_costates,
    saved_pore_load,
    saved_heat_field,
    saved_dilatation,
    saved_conductivity,
    data_residual,
    borehole_flat_position,
    probe_multiplier,
):
    step_count = saved_pore_load.shape[0]
    cells_x = closing_costates.shape[2]
    cells_y = closing_costates.shape[3]
    full_y = cells_y * lax.axis_size("gy")
    rows_x = lax.axis_index("gx") * cells_x + jnp.arange(cells_x, dtype=jnp.int32)
    cols_y = lax.axis_index("gy") * cells_y + jnp.arange(cells_y, dtype=jnp.int32)
    flat_index = rows_x[:, None] * full_y + cols_y[None, :]
    well_mask = (flat_index[None] == borehole_flat_position[:, None, None]).astype(jnp.float32)[
        ..., None
    ]
    weights = probe_multiplier.astype(jnp.float32)
    costate_vector = closing_costates
    gradient_shard = jnp.zeros(saved_pore_load.shape[1:], jnp.float32)
    for backward_counter in range(step_count - 1, -1, -1):
        pressure_now, present_heat_field, strain_now, perm_now = (
            lax.all_gather(saved_pore_load[backward_counter], "obs", axis=2, tiled=True),
            lax.all_gather(saved_heat_field[backward_counter], "obs", axis=2, tiled=True),
            lax.all_gather(saved_dilatation[backward_counter], "obs", axis=2, tiled=True),
            lax.all_gather(saved_conductivity[backward_counter], "obs", axis=2, tiled=True),
        )
        store_p = jnp.exp(strain_now)
        kept_heat_field = jnp.exp(0.5 * present_heat_field)
        coupling = 0.2 * jnp.tanh(pressure_now)
        diag_p = store_p + 6.0 * perm_now
        heat_main_entry = kept_heat_field + 6.0 * heat_diffusivity
        coeffs = (perm_now, coupling, diag_p, heat_main_entry)
        right_p = (
            store_p * costate_vector[0]
            + well_mask * data_residual[backward_counter][:, None, None, :]
        )
        heat_source_term = kept_heat_field * costate_vector[1]
        rights = jnp.stack([right_p, heat_source_term])
        for sweep_index in range(ITERS):
            costate_vector = relax_group(costate_vector, rights, coeffs)
        padded_p = padded_2(pressure_now, (("gx", 0), ("gy", 1)), 1)
        laplace = neighbour_sum(padded_p) - 6.0 * pressure_now
        weighted = jnp.sum(weights[:, None, None, None] * costate_vector[0], axis=0)
        grad_term = perm_now * laplace * weighted
        gradient_shard = gradient_shard + lax.psum_scatter(
            grad_term, "obs", scatter_dimension=2, tiled=True
        )
    return (costate_vector, gradient_shard)


def solution(mesh):
    return jax.shard_map(
        local,
        mesh=mesh,
        in_specs=(
            P(None, "obs", "gx", "gy", None),
            P(None, "gx", "gy", "obs"),
            P(None, "gx", "gy", "obs"),
            P(None, "gx", "gy", "obs"),
            P(None, "gx", "gy", "obs"),
            P(None, "obs", None),
            P("obs"),
            P("obs"),
        ),
        out_specs=(P(None, "obs", "gx", "gy", None), P("gx", "gy", "obs")),
        check_vma=False,
    )
```

profile of v0, /device:TPU:2, one launch (start us, length us, event | category | flops | bytes accessed | tf_op | source)
XLA Modules:
  0.0 513.5 jit_solution(1496356348282304289)
XLA Ops:
  9.4 4.5 collective-permute-start.1
  14.1 18.6 %all-gather.4 = f32[1,8,16,128]{2,1,0,3:T(8,128)S(1)} all-gather(f32[1,8,16,16]{2,1,0,3:T(8,128)S(1)} %copy.160), channel_id=6, replica_groups=mesh['obs'=8,'gx'=8,'gy'=4] {'obs'}, dimensions={3}, use_global_device_ids=true | all-gather | bytes 73728 | tf_op jit(solution)/shard_map/all_gather | solution.py:70
  34.7 5.5 %collective-permute-start.49 = (f32[1,16,128]{1,2,0:T(8,128)}, f32[1,16,128]{1,2,0:T(8,128)}, u32[]{:S(2)}, u32[]{:S(2)}) collective-permute-start(f32[1,16,128]{1,2,0:T(8,128)} %bitcast.18), channel_id=1, source_target_pairs={{0,4},{4,8},{8,12},{12,16},{16,20},{20,24},{24,28},{1,5},{5,9},{9,... | collective-permute-start | bytes 24584 | tf_op jit(solution)/shard_map/ppermute | solution.py:17
  40.4 15.2 %all-gather.7 = f32[1,8,16,128]{2,1,0,3:T(8,128)S(1)} all-gather(f32[1,8,16,16]{2,1,0,3:T(8,128)S(1)} %copy.163), channel_id=9, replica_groups=mesh['obs'=8,'gx'=8,'gy'=4] {'obs'}, dimensions={3}, use_global_device_ids=true | all-gather | bytes 73728 | tf_op jit(solution)/shard_map/all_gather | solution.py:70
  59.3 15.2 %all-gather.5 = f32[1,8,16,128]{2,1,0,3:T(8,128)S(1)} all-gather(f32[1,8,16,16]{2,1,0,3:T(8,128)S(1)} %copy.161), channel_id=7, replica_groups=mesh['obs'=8,'gx'=8,'gy'=4] {'obs'}, dimensions={3}, use_global_device_ids=true | all-gather | bytes 73728 | tf_op jit(solution)/shard_map/all_gather | solution.py:71
  77.0 15.1 %all-gather.10 = f32[1,8,16,128]{2,1,0,3:T(8,128)S(1)} all-gather(f32[1,8,16,16]{2,1,0,3:T(8,128)S(1)} %copy.166), channel_id=12, replica_groups=mesh['obs'=8,'gx'=8,'gy'=4] {'obs'}, dimensions={3}, use_global_device_ids=true | all-gather | bytes 73728 | tf_op jit(solution)/shard_map/all_gather | solution.py:70
  92.9 15.0 %all-gather.3 = f32[1,8,16,128]{2,1,0,3:T(8,128)S(1)} all-gather(f32[1,8,16,16]{2,1,0,3:T(8,128)S(1)} %copy.159), channel_id=5, replica_groups=mesh['obs'=8,'gx'=8,'gy'=4] {'obs'}, dimensions={3}, use_global_device_ids=true | all-gather | bytes 73728 | tf_op jit(solution)/shard_map/all_gather | solution.py:73
  108.1 15.2 %all-gather.6 = f32[1,8,16,128]{2,1,0,3:T(8,128)S(1)} all-gather(f32[1,8,16,16]{2,1,0,3:T(8,128)S(1)} %copy.162), channel_id=8, replica_groups=mesh['obs'=8,'gx'=8,'gy'=4] {'obs'}, dimensions={3}, use_global_device_ids=true | all-gather | bytes 73728 | tf_op jit(solution)/shard_map/all_gather | solution.py:73
  123.5 15.2 %all-gather.9 = f32[1,8,16,128]{2,1,0,3:T(8,128)S(1)} all-gather(f32[1,8,16,16]{2,1,0,3:T(8,128)S(1)} %copy.165), channel_id=11, replica_groups=mesh['obs'=8,'gx'=8,'gy'=4] {'obs'}, dimensions={3}, use_global_device_ids=true | all-gather | bytes 73728 | tf_op jit(solution)/shard_map/all_gather | solution.py:73
  138.8 15.2 %all-gather.2 = f32[1,8,16,128]{2,1,0,3:T(8,128)S(1)} all-gather(f32[1,8,16,16]{2,1,0,3:T(8,128)S(1)} %copy.158), channel_id=4, replica_groups=mesh['obs'=8,'gx'=8,'gy'=4] {'obs'}, dimensions={3}, use_global_device_ids=true | all-gather | bytes 73728 | tf_op jit(solution)/shard_map/all_gather | solution.py:72
  154.3 15.2 %all-gather.1 = f32[1,8,16,128]{2,1,0,3:T(8,128)S(1)} all-gather(f32[1,8,16,16]{2,1,0,3:T(8,128)S(1)} %copy.157), channel_id=3, replica_groups=mesh['obs'=8,'gx'=8,'gy'=4] {'obs'}, dimensions={3}, use_global_device_ids=true | all-gather | bytes 73728 | tf_op jit(solution)/shard_map/all_gather | solution.py:72
  169.6 15.1 %all-gather = f32[1,8,16,128]{2,1,0,3:T(8,128)S(1)} all-gather(f32[1,8,16,16]{2,1,0,3:T(8,128)S(1)} %copy.156), channel_id=2, replica_groups=mesh['obs'=8,'gx'=8,'gy'=4] {'obs'}, dimensions={3}, use_global_device_ids=true | all-gather | bytes 73728 | tf_op jit(solution)/shard_map/all_gather | solution.py:72
  189.0 3.4 collective-permute-start.3
  196.1 4.0 collective-permute-start.5
  202.1 15.1 %all-gather.8 = f32[1,8,16,128]{2,1,0,3:T(8,128)S(1)} all-gather(f32[1,8,16,16]{2,1,0,3:T(8,128)S(1)} %copy.164), channel_id=10, replica_groups=mesh['obs'=8,'gx'=8,'gy'=4] {'obs'}, dimensions={3}, use_global_device_ids=true | all-gather | bytes 73728 | tf_op jit(solution)/shard_map/all_gather | solution.py:71
  219.4 3.9 collective-permute-start.7
  225.9 7.6 %collective-permute-start.9 = (f32[2,4,1,16,128]{4,3,2,1,0:T(8,128)S(1)}, f32[2,4,1,16,128]{4,3,2,1,0:T(8,128)S(1)}, u32[]{:S(2)}, u32[]{:S(2)}) collective-permute-start(f32[2,4,1,16,128]{4,3,2,1,0:T(8,128)S(1)} %get-tuple-element.79), channel_id=1, source_target_pairs={{0,4},{4,8},{8,12},{12,16},{16,20},{20,24},{24,28},{1,5},{5,9},{9,... | collective-permute-start | bytes 196616 | tf_op jit(solution)/shard_map/ppermute | solution.py:17
  235.4 4.9 collective-permute-done.8
  242.3 3.9 collective-permute-start.11
  248.9 4.8 collective-permute-start.13
  255.8 4.0 collective-permute-done.12
  261.8 3.9 collective-permute-start.15
  268.4 3.0 collective-permute-start.17
  273.3 4.3 collective-permute-done.16
  279.6 3.9 collective-permute-start.19
  287.4 4.5 collective-permute-start.21
  295.4 16.6 %all-gather.11 = f32[1,8,16,128]{2,1,0,3:T(8,128)} all-gather(f32[1,8,16,16]{2,1,0,3:T(8,128)} %copy.167), channel_id=13, replica_groups=mesh['obs'=8,'gx'=8,'gy'=4] {'obs'}, dimensions={3}, use_global_device_ids=true | all-gather | bytes 73728 | tf_op jit(solution)/shard_map/all_gather | solution.py:71
  316.7 3.9 collective-permute-start.23
  324.6 4.6 collective-permute-start.25
  331.2 4.2 collective-permute-done.24
  337.4 3.9 collective-permute-start.27
  345.2 2.9 collective-permute-start.29
  356.3 3.9 collective-permute-start.31
  363.4 3.2 collective-permute-start.33
  368.5 5.2 %collective-permute-start.53 = (f32[1,16,128]{1,2,0:T(8,128)}, f32[1,16,128]{1,2,0:T(8,128)}, u32[]{:S(2)}, u32[]{:S(2)}) collective-permute-start(f32[1,16,128]{1,2,0:T(8,128)} %bitcast.29), channel_id=1, source_target_pairs={{0,4},{4,8},{8,12},{12,16},{16,20},{20,24},{24,28},{1,5},{5,9},{9,... | collective-permute-start | bytes 24584 | tf_op jit(solution)/shard_map/ppermute | solution.py:17
  378.8 3.9 collective-permute-start.35
  386.6 4.5 collective-permute-start.37
  393.1 5.3 %collective-permute-start.57 = (f32[1,16,128]{1,2,0:T(8,128)}, f32[1,16,128]{1,2,0:T(8,128)}, u32[]{:S(2)}, u32[]{:S(2)}) collective-permute-start(f32[1,16,128]{1,2,0:T(8,128)} %bitcast.39), channel_id=1, source_target_pairs={{0,4},{4,8},{8,12},{12,16},{16,20},{20,24},{24,28},{1,5},{5,9},{9,... | collective-permute-start | bytes 24584 | tf_op jit(solution)/shard_map/ppermute | solution.py:17
  405.3 3.9 collective-permute-start.39
  413.1 4.2 collective-permute-start.41
  419.2 3.9 collective-permute-start.51
  430.7 3.9 collective-permute-start.43
  437.3 4.7 collective-permute-start.45
  443.9 4.3 collective-permute-done.44
  450.3 3.9 collective-permute-start.47
  454.3 4.1 collective-permute-start.55
  462.6 3.9 collective-permute-start.59
  472.1 33.1 %reduce-scatter.4.cloned.1.call-done = f32[16,128]{1,0:T(8,128)} async-done(((f32[128,128]{1,0:T(8,128)}), f32[16,128]{1,0:T(8,128)}) %reduce-scatter.4.cloned.1.call-update) | async-done | bytes 8208
  (440 shorter events, 128.4 us)
Async XLA Ops:
  7.2 498.0 %reduce-scatter.4.cloned.1.call-start = ((), (), s32[]{:S(2)}) async-start(), calls=%async_computation.1 | async-start | bytes 73728
  8.1 178.3 %collective-permute-start = (f32[2,4,1,16,128]{4,3,2,1,0:T(8,128)S(1)}, f32[2,4,1,16,128]{4,3,2,1,0:T(8,128)S(1)}, u32[]{:S(2)}, u32[]{:S(2)}) collective-permute-start(f32[2,4,1,16,128]{4,3,2,1,0:T(8,128)S(1)} %get-tuple-element.83), channel_id=1, source_target_pairs={{4,0},{8,4},{12,8},{16,12},{20,16},{24,20},{28,24},{5,1},{9,5},{13... | collective-permute-start | bytes 196616 | tf_op jit(solution)/shard_map/ppermute | solution.py:18
  9.4 177.0 %collective-permute-start.1 = (f32[2,4,1,16,128]{4,3,2,1,0:T(8,128)S(1)}, f32[2,4,1,16,128]{4,3,2,1,0:T(8,128)S(1)}, u32[]{:S(2)}, u32[]{:S(2)}) collective-permute-start(f32[2,4,1,16,128]{4,3,2,1,0:T(8,128)S(1)} %get-tuple-element.84), channel_id=1, source_target_pairs={{0,4},{4,8},{8,12},{12,16},{16,20},{20,24},{24,28},{1,5},{5,9},{9,... | collective-permute-start | bytes 196616 | tf_op jit(solution)/shard_map/ppermute | solution.py:17
  33.5 335.0 %collective-permute-start.48 = (f32[1,16,128]{1,2,0:T(8,128)}, f32[1,16,128]{1,2,0:T(8,128)}, u32[]{:S(2)}, u32[]{:S(2)}) collective-permute-start(f32[1,16,128]{1,2,0:T(8,128)} %bitcast.17), channel_id=1, source_target_pairs={{4,0},{8,4},{12,8},{16,12},{20,16},{24,20},{28,24},{5,1},{9,5},{13... | collective-permute-start | bytes 24584 | tf_op jit(solution)/shard_map/ppermute | solution.py:18
  34.7 339.8 %collective-permute-start.49 = (f32[1,16,128]{1,2,0:T(8,128)}, f32[1,16,128]{1,2,0:T(8,128)}, u32[]{:S(2)}, u32[]{:S(2)}) collective-permute-start(f32[1,16,128]{1,2,0:T(8,128)} %bitcast.18), channel_id=1, source_target_pairs={{0,4},{4,8},{8,12},{12,16},{16,20},{20,24},{24,28},{1,5},{5,9},{9,... | collective-permute-start | bytes 24584 | tf_op jit(solution)/shard_map/ppermute | solution.py:17
  56.3 336.7 %collective-permute-start.52 = (f32[1,16,128]{1,2,0:T(8,128)}, f32[1,16,128]{1,2,0:T(8,128)}, u32[]{:S(2)}, u32[]{:S(2)}) collective-permute-start(f32[1,16,128]{1,2,0:T(8,128)} %bitcast.28), channel_id=1, source_target_pairs={{4,0},{8,4},{12,8},{16,12},{20,16},{24,20},{28,24},{5,1},{9,5},{13... | collective-permute-start | bytes 24584 | tf_op jit(solution)/shard_map/ppermute | solution.py:18
  186.6 6.5 %collective-permute-start.2 = (f32[2,4,10,1,128]{4,3,2,1,0:T(1,128)S(1)}, f32[2,4,10,1,128]{4,3,2,1,0:T(1,128)S(1)}, u32[]{:S(2)}, u32[]{:S(2)}) collective-permute-start(f32[2,4,10,1,128]{4,3,2,1,0:T(1,128)S(1)} %get-tuple-element.53), channel_id=1, source_target_pairs={{1,0},{2,1},{3,2},{5,4},{6,5},{7,6},{9,8},{10,9},{11,10},{13,12},{... | collective-permute-start | bytes 122888 | tf_op jit(solution)/shard_map/ppermute | solution.py:18
  196.1 21.2 %collective-permute-start.5 = (f32[2,4,1,16,128]{4,3,2,1,0:T(8,128)S(1)}, f32[2,4,1,16,128]{4,3,2,1,0:T(8,128)S(1)}, u32[]{:S(2)}, u32[]{:S(2)}) collective-permute-start(f32[2,4,1,16,128]{4,3,2,1,0:T(8,128)S(1)} %get-tuple-element.81), channel_id=1, source_target_pairs={{0,4},{4,8},{8,12},{12,16},{16,20},{20,24},{24,28},{1,5},{5,9},{9,... | collective-permute-start | bytes 196616 | tf_op jit(solution)/shard_map/ppermute | solution.py:17
  200.1 17.3 %collective-permute-start.4 = (f32[2,4,1,16,128]{4,3,2,1,0:T(8,128)S(1)}, f32[2,4,1,16,128]{4,3,2,1,0:T(8,128)S(1)}, u32[]{:S(2)}, u32[]{:S(2)}) collective-permute-start(f32[2,4,1,16,128]{4,3,2,1,0:T(8,128)S(1)} %get-tuple-element.82), channel_id=1, source_target_pairs={{4,0},{8,4},{12,8},{16,12},{20,16},{24,20},{28,24},{5,1},{9,5},{13... | collective-permute-start | bytes 196616 | tf_op jit(solution)/shard_map/ppermute | solution.py:18
  217.4 5.9 %collective-permute-start.6 = (f32[2,4,10,1,128]{4,3,2,1,0:T(1,128)S(1)}, f32[2,4,10,1,128]{4,3,2,1,0:T(1,128)S(1)}, u32[]{:S(2)}, u32[]{:S(2)}) collective-permute-start(f32[2,4,10,1,128]{4,3,2,1,0:T(1,128)S(1)} %get-tuple-element.51), channel_id=1, source_target_pairs={{1,0},{2,1},{3,2},{5,4},{6,5},{7,6},{9,8},{10,9},{11,10},{13,12},{... | collective-permute-start | bytes 122888 | tf_op jit(solution)/shard_map/ppermute | solution.py:18
  225.9 9.5 %collective-permute-start.9 = (f32[2,4,1,16,128]{4,3,2,1,0:T(8,128)S(1)}, f32[2,4,1,16,128]{4,3,2,1,0:T(8,128)S(1)}, u32[]{:S(2)}, u32[]{:S(2)}) collective-permute-start(f32[2,4,1,16,128]{4,3,2,1,0:T(8,128)S(1)} %get-tuple-element.79), channel_id=1, source_target_pairs={{0,4},{4,8},{8,12},{12,16},{16,20},{20,24},{24,28},{1,5},{5,9},{9,... | collective-permute-start | bytes 196616 | tf_op jit(solution)/shard_map/ppermute | solution.py:17
  233.5 6.8 %collective-permute-start.8 = (f32[2,4,1,16,128]{4,3,2,1,0:T(8,128)S(1)}, f32[2,4,1,16,128]{4,3,2,1,0:T(8,128)S(1)}, u32[]{:S(2)}, u32[]{:S(2)}) collective-permute-start(f32[2,4,1,16,128]{4,3,2,1,0:T(8,128)S(1)} %get-tuple-element.80), channel_id=1, source_target_pairs={{4,0},{8,4},{12,8},{16,12},{20,16},{24,20},{28,24},{5,1},{9,5},{13... | collective-permute-start | bytes 196616 | tf_op jit(solution)/shard_map/ppermute | solution.py:18
  240.4 5.9 %collective-permute-start.10 = (f32[2,4,10,1,128]{4,3,2,1,0:T(1,128)S(1)}, f32[2,4,10,1,128]{4,3,2,1,0:T(1,128)S(1)}, u32[]{:S(2)}, u32[]{:S(2)}) collective-permute-start(f32[2,4,10,1,128]{4,3,2,1,0:T(1,128)S(1)} %get-tuple-element.49), channel_id=1, source_target_pairs={{1,0},{2,1},{3,2},{5,4},{6,5},{7,6},{9,8},{10,9},{11,10},{13,12},{... | collective-permute-start | bytes 122888 | tf_op jit(solution)/shard_map/ppermute | solution.py:18
  248.9 6.9 %collective-permute-start.13 = (f32[2,4,1,16,128]{4,3,2,1,0:T(8,128)S(1)}, f32[2,4,1,16,128]{4,3,2,1,0:T(8,128)S(1)}, u32[]{:S(2)}, u32[]{:S(2)}) collective-permute-start(f32[2,4,1,16,128]{4,3,2,1,0:T(8,128)S(1)} %get-tuple-element.77), channel_id=1, source_target_pairs={{0,4},{4,8},{8,12},{12,16},{16,20},{20,24},{24,28},{1,5},{5,9},{9,... | collective-permute-start | bytes 196616 | tf_op jit(solution)/shard_map/ppermute | solution.py:17
  253.7 6.2 %collective-permute-start.12 = (f32[2,4,1,16,128]{4,3,2,1,0:T(8,128)S(1)}, f32[2,4,1,16,128]{4,3,2,1,0:T(8,128)S(1)}, u32[]{:S(2)}, u32[]{:S(2)}) collective-permute-start(f32[2,4,1,16,128]{4,3,2,1,0:T(8,128)S(1)} %get-tuple-element.78), channel_id=1, source_target_pairs={{4,0},{8,4},{12,8},{16,12},{20,16},{24,20},{28,24},{5,1},{9,5},{13... | collective-permute-start | bytes 196616 | tf_op jit(solution)/shard_map/ppermute | solution.py:18
  259.9 5.9 %collective-permute-start.14 = (f32[2,4,10,1,128]{4,3,2,1,0:T(1,128)S(1)}, f32[2,4,10,1,128]{4,3,2,1,0:T(1,128)S(1)}, u32[]{:S(2)}, u32[]{:S(2)}) collective-permute-start(f32[2,4,10,1,128]{4,3,2,1,0:T(1,128)S(1)} %get-tuple-element.47), channel_id=1, source_target_pairs={{1,0},{2,1},{3,2},{5,4},{6,5},{7,6},{9,8},{10,9},{11,10},{13,12},{... | collective-permute-start | bytes 122888 | tf_op jit(solution)/shard_map/ppermute | solution.py:18
  271.4 6.2 %collective-permute-start.16 = (f32[2,4,1,16,128]{4,3,2,1,0:T(8,128)S(1)}, f32[2,4,1,16,128]{4,3,2,1,0:T(8,128)S(1)}, u32[]{:S(2)}, u32[]{:S(2)}) collective-permute-start(f32[2,4,1,16,128]{4,3,2,1,0:T(8,128)S(1)} %get-tuple-element.76), channel_id=1, source_target_pairs={{4,0},{8,4},{12,8},{16,12},{20,16},{24,20},{28,24},{5,1},{9,5},{13... | collective-permute-start | bytes 196616 | tf_op jit(solution)/shard_map/ppermute | solution.py:18
  277.7 5.9 %collective-permute-start.18 = (f32[2,4,10,1,128]{4,3,2,1,0:T(1,128)S(1)}, f32[2,4,10,1,128]{4,3,2,1,0:T(1,128)S(1)}, u32[]{:S(2)}, u32[]{:S(2)}) collective-permute-start(f32[2,4,10,1,128]{4,3,2,1,0:T(1,128)S(1)} %get-tuple-element.45), channel_id=1, source_target_pairs={{1,0},{2,1},{3,2},{5,4},{6,5},{7,6},{9,8},{10,9},{11,10},{13,12},{... | collective-permute-start | bytes 122888 | tf_op jit(solution)/shard_map/ppermute | solution.py:18
  287.4 26.4 %collective-permute-start.21 = (f32[2,4,1,16,128]{4,3,2,1,0:T(8,128)}, f32[2,4,1,16,128]{4,3,2,1,0:T(8,128)}, u32[]{:S(2)}, u32[]{:S(2)}) collective-permute-start(f32[2,4,1,16,128]{4,3,2,1,0:T(8,128)} %get-tuple-element.73), channel_id=1, source_target_pairs={{0,4},{4,8},{8,12},{12,16},{16,20},{20,24},{24,28},{1,5},{5,9},{9,... | collective-permute-start | bytes 196616 | tf_op jit(solution)/shard_map/ppermute | solution.py:17
  291.9 22.0 %collective-permute-start.20 = (f32[2,4,1,16,128]{4,3,2,1,0:T(8,128)}, f32[2,4,1,16,128]{4,3,2,1,0:T(8,128)}, u32[]{:S(2)}, u32[]{:S(2)}) collective-permute-start(f32[2,4,1,16,128]{4,3,2,1,0:T(8,128)} %get-tuple-element.74), channel_id=1, source_target_pairs={{4,0},{8,4},{12,8},{16,12},{20,16},{24,20},{28,24},{5,1},{9,5},{13... | collective-permute-start | bytes 196616 | tf_op jit(solution)/shard_map/ppermute | solution.py:18
  314.7 6.0 %collective-permute-start.22 = (f32[2,4,10,1,128]{4,3,2,1,0:T(1,128)S(1)}, f32[2,4,10,1,128]{4,3,2,1,0:T(1,128)S(1)}, u32[]{:S(2)}, u32[]{:S(2)}) collective-permute-start(f32[2,4,10,1,128]{4,3,2,1,0:T(1,128)S(1)} %get-tuple-element.43), channel_id=1, source_target_pairs={{1,0},{2,1},{3,2},{5,4},{6,5},{7,6},{9,8},{10,9},{11,10},{13,12},{... | collective-permute-start | bytes 122888 | tf_op jit(solution)/shard_map/ppermute | solution.py:18
  324.6 6.6 %collective-permute-start.25 = (f32[2,4,1,16,128]{4,3,2,1,0:T(8,128)S(1)}, f32[2,4,1,16,128]{4,3,2,1,0:T(8,128)S(1)}, u32[]{:S(2)}, u32[]{:S(2)}) collective-permute-start(f32[2,4,1,16,128]{4,3,2,1,0:T(8,128)S(1)} %get-tuple-element.71), channel_id=1, source_target_pairs={{0,4},{4,8},{8,12},{12,16},{16,20},{20,24},{24,28},{1,5},{5,9},{9,... | collective-permute-start | bytes 196616 | tf_op jit(solution)/shard_map/ppermute | solution.py:17
  329.3 6.2 %collective-permute-start.24 = (f32[2,4,1,16,128]{4,3,2,1,0:T(8,128)S(1)}, f32[2,4,1,16,128]{4,3,2,1,0:T(8,128)S(1)}, u32[]{:S(2)}, u32[]{:S(2)}) collective-permute-start(f32[2,4,1,16,128]{4,3,2,1,0:T(8,128)S(1)} %get-tuple-element.72), channel_id=1, source_target_pairs={{4,0},{8,4},{12,8},{16,12},{20,16},{24,20},{28,24},{5,1},{9,5},{13... | collective-permute-start | bytes 196616 | tf_op jit(solution)/shard_map/ppermute | solution.py:18
  335.5 5.9 %collective-permute-start.26 = (f32[2,4,10,1,128]{4,3,2,1,0:T(1,128)S(1)}, f32[2,4,10,1,128]{4,3,2,1,0:T(1,128)S(1)}, u32[]{:S(2)}, u32[]{:S(2)}) collective-permute-start(f32[2,4,10,1,128]{4,3,2,1,0:T(1,128)S(1)} %get-tuple-element.41), channel_id=1, source_target_pairs={{1,0},{2,1},{3,2},{5,4},{6,5},{7,6},{9,8},{10,9},{11,10},{13,12},{... | collective-permute-start | bytes 122888 | tf_op jit(solution)/shard_map/ppermute | solution.py:18
  345.2 6.7 %collective-permute-start.29 = (f32[2,4,1,16,128]{4,3,2,1,0:T(8,128)}, f32[2,4,1,16,128]{4,3,2,1,0:T(8,128)S(1)}, u32[]{:S(2)}, u32[]{:S(2)}) collective-permute-start(f32[2,4,1,16,128]{4,3,2,1,0:T(8,128)} %get-tuple-element.69), channel_id=1, source_target_pairs={{0,4},{4,8},{8,12},{12,16},{16,20},{20,24},{24,28},{1,5},{5,9},{9,... | collective-permute-start | bytes 196616 | tf_op jit(solution)/shard_map/ppermute | solution.py:17
  348.1 6.2 %collective-permute-start.28 = (f32[2,4,1,16,128]{4,3,2,1,0:T(8,128)S(1)}, f32[2,4,1,16,128]{4,3,2,1,0:T(8,128)S(1)}, u32[]{:S(2)}, u32[]{:S(2)}) collective-permute-start(f32[2,4,1,16,128]{4,3,2,1,0:T(8,128)S(1)} %get-tuple-element.70), channel_id=1, source_target_pairs={{4,0},{8,4},{12,8},{16,12},{20,16},{24,20},{28,24},{5,1},{9,5},{13... | collective-permute-start | bytes 196616 | tf_op jit(solution)/shard_map/ppermute | solution.py:18
  354.3 6.0 %collective-permute-start.30 = (f32[2,4,10,1,128]{4,3,2,1,0:T(1,128)S(1)}, f32[2,4,10,1,128]{4,3,2,1,0:T(1,128)S(1)}, u32[]{:S(2)}, u32[]{:S(2)}) collective-permute-start(f32[2,4,10,1,128]{4,3,2,1,0:T(1,128)S(1)} %get-tuple-element.39), channel_id=1, source_target_pairs={{1,0},{2,1},{3,2},{5,4},{6,5},{7,6},{9,8},{10,9},{11,10},{13,12},{... | collective-permute-start | bytes 122888 | tf_op jit(solution)/shard_map/ppermute | solution.py:18
  363.4 13.3 %collective-permute-start.33 = (f32[2,4,1,16,128]{4,3,2,1,0:T(8,128)S(1)}, f32[2,4,1,16,128]{4,3,2,1,0:T(8,128)S(1)}, u32[]{:S(2)}, u32[]{:S(2)}) collective-permute-start(f32[2,4,1,16,128]{4,3,2,1,0:T(8,128)S(1)} %get-tuple-element.67), channel_id=1, source_target_pairs={{0,4},{4,8},{8,12},{12,16},{16,20},{20,24},{24,28},{1,5},{5,9},{9,... | collective-permute-start | bytes 196616 | tf_op jit(solution)/shard_map/ppermute | solution.py:17
  366.6 10.1 %collective-permute-start.32 = (f32[2,4,1,16,128]{4,3,2,1,0:T(8,128)S(1)}, f32[2,4,1,16,128]{4,3,2,1,0:T(8,128)S(1)}, u32[]{:S(2)}, u32[]{:S(2)}) collective-permute-start(f32[2,4,1,16,128]{4,3,2,1,0:T(8,128)S(1)} %get-tuple-element.68), channel_id=1, source_target_pairs={{4,0},{8,4},{12,8},{16,12},{20,16},{24,20},{28,24},{5,1},{9,5},{13... | collective-permute-start | bytes 196616 | tf_op jit(solution)/shard_map/ppermute | solution.py:18
  368.5 31.4 %collective-permute-start.53 = (f32[1,16,128]{1,2,0:T(8,128)}, f32[1,16,128]{1,2,0:T(8,128)}, u32[]{:S(2)}, u32[]{:S(2)}) collective-permute-start(f32[1,16,128]{1,2,0:T(8,128)} %bitcast.29), channel_id=1, source_target_pairs={{0,4},{4,8},{8,12},{12,16},{16,20},{20,24},{24,28},{1,5},{5,9},{9,... | collective-permute-start | bytes 24584 | tf_op jit(solution)/shard_map/ppermute | solution.py:17
  374.6 44.7 %collective-permute-start.56 = (f32[1,16,128]{1,2,0:T(8,128)}, f32[1,16,128]{1,2,0:T(8,128)}, u32[]{:S(2)}, u32[]{:S(2)}) collective-permute-start(f32[1,16,128]{1,2,0:T(8,128)} %bitcast.38), channel_id=1, source_target_pairs={{4,0},{8,4},{12,8},{16,12},{20,16},{24,20},{28,24},{5,1},{9,5},{13... | collective-permute-start | bytes 24584 | tf_op jit(solution)/shard_map/ppermute | solution.py:18
  376.9 5.9 %collective-permute-start.34 = (f32[2,4,10,1,128]{4,3,2,1,0:T(1,128)S(1)}, f32[2,4,10,1,128]{4,3,2,1,0:T(1,128)S(1)}, u32[]{:S(2)}, u32[]{:S(2)}) collective-permute-start(f32[2,4,10,1,128]{4,3,2,1,0:T(1,128)S(1)} %get-tuple-element.37), channel_id=1, source_target_pairs={{1,0},{2,1},{3,2},{5,4},{6,5},{7,6},{9,8},{10,9},{11,10},{13,12},{... | collective-permute-start | bytes 122888 | tf_op jit(solution)/shard_map/ppermute | solution.py:18
  386.6 16.7 %collective-permute-start.37 = (f32[2,4,1,16,128]{4,3,2,1,0:T(8,128)}, f32[2,4,1,16,128]{4,3,2,1,0:T(8,128)S(1)}, u32[]{:S(2)}, u32[]{:S(2)}) collective-permute-start(f32[2,4,1,16,128]{4,3,2,1,0:T(8,128)} %get-tuple-element.65), channel_id=1, source_target_pairs={{0,4},{4,8},{8,12},{12,16},{16,20},{20,24},{24,28},{1,5},{5,9},{9,... | collective-permute-start | bytes 196616 | tf_op jit(solution)/shard_map/ppermute | solution.py:17
  391.1 12.2 %collective-permute-start.36 = (f32[2,4,1,16,128]{4,3,2,1,0:T(8,128)S(1)}, f32[2,4,1,16,128]{4,3,2,1,0:T(8,128)S(1)}, u32[]{:S(2)}, u32[]{:S(2)}) collective-permute-start(f32[2,4,1,16,128]{4,3,2,1,0:T(8,128)S(1)} %get-tuple-element.66), channel_id=1, source_target_pairs={{4,0},{8,4},{12,8},{16,12},{20,16},{24,20},{28,24},{5,1},{9,5},{13... | collective-permute-start | bytes 196616 | tf_op jit(solution)/shard_map/ppermute | solution.py:18
  393.1 31.6 %collective-permute-start.57 = (f32[1,16,128]{1,2,0:T(8,128)}, f32[1,16,128]{1,2,0:T(8,128)}, u32[]{:S(2)}, u32[]{:S(2)}) collective-permute-start(f32[1,16,128]{1,2,0:T(8,128)} %bitcast.39), channel_id=1, source_target_pairs={{0,4},{4,8},{8,12},{12,16},{16,20},{20,24},{24,28},{1,5},{5,9},{9,... | collective-permute-start | bytes 24584 | tf_op jit(solution)/shard_map/ppermute | solution.py:17
  399.9 62.7 %collective-permute-start.50 = (f32[10,1,128]{2,1,0:T(1,128)}, f32[10,1,128]{2,1,0:T(1,128)}, u32[]{:S(2)}, u32[]{:S(2)}) collective-permute-start(f32[10,1,128]{2,1,0:T(1,128)} %get-tuple-element.97), channel_id=1, source_target_pairs={{1,0},{2,1},{3,2},{5,4},{6,5},{7,6},{9,8},{10,9},{11,10},{13,12},{... | collective-permute-start | bytes 15368 | tf_op jit(solution)/shard_map/ppermute | solution.py:18
  403.4 6.0 %collective-permute-start.38 = (f32[2,4,10,1,128]{4,3,2,1,0:T(1,128)S(1)}, f32[2,4,10,1,128]{4,3,2,1,0:T(1,128)S(1)}, u32[]{:S(2)}, u32[]{:S(2)}) collective-permute-start(f32[2,4,10,1,128]{4,3,2,1,0:T(1,128)S(1)} %get-tuple-element.35), channel_id=1, source_target_pairs={{1,0},{2,1},{3,2},{5,4},{6,5},{7,6},{9,8},{10,9},{11,10},{13,12},{... | collective-permute-start | bytes 122888 | tf_op jit(solution)/shard_map/ppermute | solution.py:18
  413.1 15.6 %collective-permute-start.41 = (f32[2,4,1,16,128]{4,3,2,1,0:T(8,128)}, f32[2,4,1,16,128]{4,3,2,1,0:T(8,128)S(1)}, u32[]{:S(2)}, u32[]{:S(2)}) collective-permute-start(f32[2,4,1,16,128]{4,3,2,1,0:T(8,128)} %get-tuple-element.63), channel_id=1, source_target_pairs={{0,4},{4,8},{8,12},{12,16},{16,20},{20,24},{24,28},{1,5},{5,9},{9,... | collective-permute-start | bytes 196616 | tf_op jit(solution)/shard_map/ppermute | solution.py:17
  417.3 11.4 %collective-permute-start.40 = (f32[2,4,1,16,128]{4,3,2,1,0:T(8,128)}, f32[2,4,1,16,128]{4,3,2,1,0:T(8,128)S(1)}, u32[]{:S(2)}, u32[]{:S(2)}) collective-permute-start(f32[2,4,1,16,128]{4,3,2,1,0:T(8,128)} %get-tuple-element.64), channel_id=1, source_target_pairs={{4,0},{8,4},{12,8},{16,12},{20,16},{24,20},{28,24},{5,1},{9,5},{13... | collective-permute-start | bytes 196616 | tf_op jit(solution)/shard_map/ppermute | solution.py:18
  419.2 47.5 %collective-permute-start.51 = (f32[10,1,128]{2,1,0:T(1,128)}, f32[10,1,128]{2,1,0:T(1,128)}, u32[]{:S(2)}, u32[]{:S(2)}) collective-permute-start(f32[10,1,128]{2,1,0:T(1,128)} %get-tuple-element.98), channel_id=1, source_target_pairs={{0,1},{1,2},{2,3},{4,5},{5,6},{6,7},{8,9},{9,10},{10,11},{12,13},{... | collective-permute-start | bytes 15368 | tf_op jit(solution)/shard_map/ppermute | solution.py:17
  424.7 42.0 %collective-permute-start.54 = (f32[10,1,128]{2,1,0:T(1,128)}, f32[10,1,128]{2,1,0:T(1,128)}, u32[]{:S(2)}, u32[]{:S(2)}) collective-permute-start(f32[10,1,128]{2,1,0:T(1,128)} %get-tuple-element.99), channel_id=1, source_target_pairs={{1,0},{2,1},{3,2},{5,4},{6,5},{7,6},{9,8},{10,9},{11,10},{13,12},{... | collective-permute-start | bytes 15368 | tf_op jit(solution)/shard_map/ppermute | solution.py:18
  428.7 6.0 %collective-permute-start.42 = (f32[2,4,10,1,128]{4,3,2,1,0:T(1,128)S(1)}, f32[2,4,10,1,128]{4,3,2,1,0:T(1,128)S(1)}, u32[]{:S(2)}, u32[]{:S(2)}) collective-permute-start(f32[2,4,10,1,128]{4,3,2,1,0:T(1,128)S(1)} %get-tuple-element.33), channel_id=1, source_target_pairs={{1,0},{2,1},{3,2},{5,4},{6,5},{7,6},{9,8},{10,9},{11,10},{13,12},{... | collective-permute-start | bytes 122888 | tf_op jit(solution)/shard_map/ppermute | solution.py:18
  437.3 6.6 %collective-permute-start.45 = (f32[2,4,1,16,128]{4,3,2,1,0:T(8,128)S(1)}, f32[2,4,1,16,128]{4,3,2,1,0:T(8,128)S(1)}, u32[]{:S(2)}, u32[]{:S(2)}) collective-permute-start(f32[2,4,1,16,128]{4,3,2,1,0:T(8,128)S(1)} %get-tuple-element.61), channel_id=1, source_target_pairs={{0,4},{4,8},{8,12},{12,16},{16,20},{20,24},{24,28},{1,5},{5,9},{9,... | collective-permute-start | bytes 196616 | tf_op jit(solution)/shard_map/ppermute | solution.py:17
  442.0 6.2 %collective-permute-start.44 = (f32[2,4,1,16,128]{4,3,2,1,0:T(8,128)S(1)}, f32[2,4,1,16,128]{4,3,2,1,0:T(8,128)S(1)}, u32[]{:S(2)}, u32[]{:S(2)}) collective-permute-start(f32[2,4,1,16,128]{4,3,2,1,0:T(8,128)S(1)} %get-tuple-element.62), channel_id=1, source_target_pairs={{4,0},{8,4},{12,8},{16,12},{20,16},{24,20},{28,24},{5,1},{9,5},{13... | collective-permute-start | bytes 196616 | tf_op jit(solution)/shard_map/ppermute | solution.py:18
  448.3 6.1 %collective-permute-start.46 = (f32[2,4,10,1,128]{4,3,2,1,0:T(1,128)S(1)}, f32[2,4,10,1,128]{4,3,2,1,0:T(1,128)S(1)}, u32[]{:S(2)}, u32[]{:S(2)}) collective-permute-start(f32[2,4,10,1,128]{4,3,2,1,0:T(1,128)S(1)} %get-tuple-element.31), channel_id=1, source_target_pairs={{1,0},{2,1},{3,2},{5,4},{6,5},{7,6},{9,8},{10,9},{11,10},{13,12},{... | collective-permute-start | bytes 122888 | tf_op jit(solution)/shard_map/ppermute | solution.py:18
  450.3 8.1 %collective-permute-start.47 = (f32[2,4,10,1,128]{4,3,2,1,0:T(1,128)S(1)}, f32[2,4,10,1,128]{4,3,2,1,0:T(1,128)S(1)}, u32[]{:S(2)}, u32[]{:S(2)}) collective-permute-start(f32[2,4,10,1,128]{4,3,2,1,0:T(1,128)S(1)} %get-tuple-element.32), channel_id=1, source_target_pairs={{0,1},{1,2},{2,3},{4,5},{5,6},{6,7},{8,9},{9,10},{10,11},{12,13},{... | collective-permute-start | bytes 122888 | tf_op jit(solution)/shard_map/ppermute | solution.py:17
  454.3 12.4 %collective-permute-start.55 = (f32[10,1,128]{2,1,0:T(1,128)S(1)}, f32[10,1,128]{2,1,0:T(1,128)S(1)}, u32[]{:S(2)}, u32[]{:S(2)}) collective-permute-start(f32[10,1,128]{2,1,0:T(1,128)S(1)} %copy-done.107), channel_id=1, source_target_pairs={{0,1},{1,2},{2,3},{4,5},{5,6},{6,7},{8,9},{9,10},{10,11},{12,13},{... | collective-permute-start | bytes 15368 | tf_op jit(solution)/shard_map/ppermute | solution.py:17
  458.5 8.2 %collective-permute-start.58 = (f32[10,1,128]{2,1,0:T(1,128)S(1)}, f32[10,1,128]{2,1,0:T(1,128)S(1)}, u32[]{:S(2)}, u32[]{:S(2)}) collective-permute-start(f32[10,1,128]{2,1,0:T(1,128)S(1)} %get-tuple-element.101), channel_id=1, source_target_pairs={{1,0},{2,1},{3,2},{5,4},{6,5},{7,6},{9,8},{10,9},{11,10},{13,12},{... | collective-permute-start | bytes 15368 | tf_op jit(solution)/shard_map/ppermute | solution.py:18
  (124 other events, 1643.9 us)
Sparse Core Ops, SparseCore 0:
  470.3 34.7 reduce-scatter.3
where the time goes:
time: 516 us; the launch traced here: 513 us
  blocking collectives  187 us (36%)
  starting transfers between devices  177 us (34%)
  waiting for transfers between devices  80.4 us (16%)
  local copies, waits for them, and re-layouts  31.7 us (6%)
  other arithmetic  21.6 us (4%)
  between operations  16.7 us (3%)
    ppermute x30, starting transfers between devices, padded_2(): before = lax.ppermute(last, axis, up)  127 us
    ppermute x30, starting transfers between devices, padded_2(): after = lax.ppermute(initial, axis, down)  49.5 us
    all_gather x3, blocking collectives, local(): lax.all_gather(saved_pore_load[backward_counter], 'obs', axis=2, tiled=True)  48.9 us
    all_gather x3, blocking collectives, local(): lax.all_gather(saved_heat_field[backward_counter], 'obs', axis=2, tiled=T...  46.9 us
    all_gather x3, blocking collectives, local(): lax.all_gather(saved_dilatation[backward_counter], 'obs', axis=2, tiled=T...  45.5 us
    all_gather x3, blocking collectives, local(): lax.all_gather(saved_conductivity[backward_counter], 'obs', axis=2, tiled...  45.3 us
    unnamed x2, waiting for transfers between devices  33.1 us
    ppermute x30, waiting for transfers between devices, padded_2(): after = lax.ppermute(initial, axis, down)  24.2 us
  transfers between devices with their start and end apart: 61, of which 22 were waited for; matrix products, arithmetic and copies ran while one was open for 8% of the time, Pallas kernels for 0%

commit v1 on v0

--- a/solution.py
+++ b/solution.py
@@ -5,6 +5,13 @@
 
 ITERS = 4
 heat_diffusivity = 2.0
+
+
+def exchange_gather(x, name, dim):
+    n_dev = lax.axis_size(name)
+    blocks = jnp.stack([x for _ in range(n_dev)])
+    blocks = lax.all_to_all(blocks, name, split_axis=0, concat_axis=0)
+    return jnp.concatenate(blocks, axis=dim)
 
 
 def padded_2(value, sides, width):
@@ -69,7 +76,7 @@
         pressure_now, present_heat_field, strain_now, perm_now = (
             lax.all_gather(saved_pore_load[backward_counter], "obs", axis=2, tiled=True),
             lax.all_gather(saved_heat_field[backward_counter], "obs", axis=2, tiled=True),
-            lax.all_gather(saved_dilatation[backward_counter], "obs", axis=2, tiled=True),
+            exchange_gather(saved_dilatation[backward_counter], "obs", 2),
             lax.all_gather(saved_conductivity[backward_counter], "obs", axis=2, tiled=True),
         )
         store_p = jnp.exp(strain_now)

time: 516 us -> 487 us (0.944)
  blocking collectives: 187 us -> 145 us
  starting transfers between devices: 177 us -> 207 us
  waiting for transfers between devices: 80.4 us -> 68.9 us
  local copies, waits for them, and re-layouts: 31.7 us -> 25.8 us
    all_gather x3 -> x0, blocking collectives: 45.5 us -> none  [local(): lax.all_gather(saved_dilatation[backward_counter], 'obs', axis=2, tiled=T...]
    ppermute x30, waiting for transfers between devices: 24.2 us -> 1.07 us  [padded_2(): after = lax.ppermute(initial, axis, down)]
    all_to_all x0 -> x3, starting transfers between devices: none -> 16.4 us  [exchange_gather(): blocks = lax.all_to_all(blocks, name, split_axis=0, concat_axis=0)]
    ppermute x30, starting transfers between devices: 127 us -> 140 us  [padded_2(): before = lax.ppermute(last, axis, up)]
    unnamed x2, waiting for transfers between devices: 33.1 us -> 42 us
    ppermute x6 -> x0, local copies, waits for them, and re-layouts: 7.8 us -> none  [the longest x3 3.9 us: padded_2(): before = lax.ppermute(last, axis, up)]
    all_gather x3, blocking collectives: 45.3 us -> 51.5 us  [local(): lax.all_gather(saved_conductivity[backward_counter], 'obs', axis=2, tiled...]
    unnamed x240 -> x181, local copies, waits for them, and re-layouts: 12.5 us -> 12.8 us
  transfers between devices with their start and end apart: 61 -> 64, of which waited for: 22 -> 21; matrix products, arithmetic and copies ran while one was open for 8% -> 8% of each run, Pallas kernels for 0% -> 0%
where the time goes in v1:
time: 487 us; the launch traced here: 484 us
  starting transfers between devices  207 us (43%)
  blocking collectives  145 us (30%)
  waiting for transfers between devices  68.9 us (14%)
  local copies, waits for them, and re-layouts  25.8 us (5%)
  other arithmetic  21.3 us (4%)
  between operations  16.5 us (3%)
    ppermute x30, starting transfers between devices, padded_2(): before = lax.ppermute(last, axis, up)  140 us
    all_gather x3, blocking collectives, local(): lax.all_gather(saved_conductivity[backward_counter], 'obs', axis=2, tiled...  51.5 us
    ppermute x30, starting transfers between devices, padded_2(): after = lax.ppermute(initial, axis, down)  49.9 us
    all_gather x3, blocking collectives, local(): lax.all_gather(saved_pore_load[backward_counter], 'obs', axis=2, tiled=True)  48 us
    all_gather x3, blocking collectives, local(): lax.all_gather(saved_heat_field[backward_counter], 'obs', axis=2, tiled=T...  45.4 us
    unnamed x2, waiting for transfers between devices  42 us
    ppermute x30, waiting for transfers between devices, padded_2(): before = lax.ppermute(last, axis, up)  25.7 us
    all_to_all x3, starting transfers between devices, exchange_gather(): blocks = lax.all_to_all(blocks, name, split_axis=0, concat_axis=0)  16.4 us
  transfers between devices with their start and end apart: 64, of which 21 were waited for; matrix products, arithmetic and copies ran while one was open for 8% of the time, Pallas kernels for 0%

profile of v1, /device:TPU:2, one launch (start us, length us, event | category | flops | bytes accessed | tf_op | source)
XLA Modules:
  0.0 484.0 jit_solution(13847571004765425254)
XLA Ops:
  8.1 3.8 collective-permute-start.1
  14.2 7.6 %all-to-all-start.2 = ((f32[8,1,2048]{2,1,0:T(1,128)}), f32[8,1,2048]{2,1,0:T(1,128)S(1)}, u32[]{:S(2)}, u32[]{:S(2)}) async-start(f32[8,1,2048]{2,1,0:T(1,128)} %reshape.147), calls=%async_computation.2 | async-start | bytes 131072 | tf_op jit(solution)/shard_map/all_to_all | solution.py:13
  21.9 17.6 %all-gather.1 = f32[1,8,16,128]{2,1,0,3:T(8,128)S(1)} all-gather(f32[1,8,16,16]{2,1,0,3:T(8,128)S(1)} %copy.134), channel_id=3, replica_groups=mesh['obs'=8,'gx'=8,'gy'=4] {'obs'}, dimensions={3}, use_global_device_ids=true | all-gather | bytes 73728 | tf_op jit(solution)/shard_map/all_gather | solution.py:77
  41.6 5.6 %collective-permute-start.49 = (f32[1,16,128]{2,1,0:T(8,128)}, f32[1,16,128]{2,1,0:T(8,128)}, u32[]{:S(2)}, u32[]{:S(2)}) collective-permute-start(f32[1,16,128]{2,1,0:T(8,128)} %get-tuple-element.97), channel_id=1, source_target_pairs={{0,4},{4,8},{8,12},{12,16},{16,20},{20,24},{24,28},{1,5},{5,9},{9,... | collective-permute-start | bytes 24584 | tf_op jit(solution)/shard_map/ppermute | solution.py:24
  47.3 15.2 %all-gather.4 = f32[1,8,16,128]{2,1,0,3:T(8,128)S(1)} all-gather(f32[1,8,16,16]{2,1,0,3:T(8,128)S(1)} %copy.137), channel_id=6, replica_groups=mesh['obs'=8,'gx'=8,'gy'=4] {'obs'}, dimensions={3}, use_global_device_ids=true | all-gather | bytes 73728 | tf_op jit(solution)/shard_map/all_gather | solution.py:77
  64.8 15.1 %all-gather.2 = f32[1,8,16,128]{2,1,0,3:T(8,128)S(1)} all-gather(f32[1,8,16,16]{2,1,0,3:T(8,128)S(1)} %copy.135), channel_id=4, replica_groups=mesh['obs'=8,'gx'=8,'gy'=4] {'obs'}, dimensions={3}, use_global_device_ids=true | all-gather | bytes 73728 | tf_op jit(solution)/shard_map/all_gather | solution.py:78
  81.0 15.2 %all-gather.5 = f32[1,8,16,128]{2,1,0,3:T(8,128)S(1)} all-gather(f32[1,8,16,16]{2,1,0,3:T(8,128)S(1)} %copy.138), channel_id=7, replica_groups=mesh['obs'=8,'gx'=8,'gy'=4] {'obs'}, dimensions={3}, use_global_device_ids=true | all-gather | bytes 73728 | tf_op jit(solution)/shard_map/all_gather | solution.py:78
  100.5 2.4 collective-permute-start.2
  103.0 3.4 collective-permute-start.3
  106.4 15.2 %all-gather = f32[1,8,16,128]{2,1,0,3:T(8,128)S(1)} all-gather(f32[1,8,16,16]{2,1,0,3:T(8,128)S(1)} %copy.133), channel_id=2, replica_groups=mesh['obs'=8,'gx'=8,'gy'=4] {'obs'}, dimensions={3}, use_global_device_ids=true | all-gather | bytes 73728 | tf_op jit(solution)/shard_map/all_gather | solution.py:80
  122.8 15.0 %all-gather.8 = f32[1,8,16,128]{2,1,0,3:T(8,128)S(1)} all-gather(f32[1,8,16,16]{2,1,0,3:T(8,128)S(1)} %copy.141), channel_id=10, replica_groups=mesh['obs'=8,'gx'=8,'gy'=4] {'obs'}, dimensions={3}, use_global_device_ids=true | all-gather | bytes 73728 | tf_op jit(solution)/shard_map/all_gather | solution.py:78
  138.4 4.5 all-to-all-start.1
  146.5 6.0 %collective-permute-start.5 = (f32[2,4,1,16,128]{4,3,2,1,0:T(8,128)S(1)}, f32[2,4,1,16,128]{4,3,2,1,0:T(8,128)S(1)}, u32[]{:S(2)}, u32[]{:S(2)}) collective-permute-start(f32[2,4,1,16,128]{4,3,2,1,0:T(8,128)S(1)} %get-tuple-element.75), channel_id=1, source_target_pairs={{0,4},{4,8},{8,12},{12,16},{16,20},{20,24},{24,28},{1,5},{5,9},{9,... | collective-permute-start | bytes 196616 | tf_op jit(solution)/shard_map/ppermute | solution.py:24
  154.6 2.4 collective-permute-start.6
  157.0 3.4 collective-permute-start.7
  160.5 2.4 collective-permute-done.7
  164.8 5.4 %collective-permute-start.9 = (f32[2,4,1,16,128]{4,3,2,1,0:T(8,128)S(1)}, f32[2,4,1,16,128]{4,3,2,1,0:T(8,128)S(1)}, u32[]{:S(2)}, u32[]{:S(2)}) collective-permute-start(f32[2,4,1,16,128]{4,3,2,1,0:T(8,128)S(1)} %get-tuple-element.73), channel_id=1, source_target_pairs={{0,4},{4,8},{8,12},{12,16},{16,20},{20,24},{24,28},{1,5},{5,9},{9,... | collective-permute-start | bytes 196616 | tf_op jit(solution)/shard_map/ppermute | solution.py:24
  170.9 17.6 %all-gather.3 = f32[1,8,16,128]{2,1,0,3:T(8,128)S(1)} all-gather(f32[1,8,16,16]{2,1,0,3:T(8,128)S(1)} %copy.136), channel_id=5, replica_groups=mesh['obs'=8,'gx'=8,'gy'=4] {'obs'}, dimensions={3}, use_global_device_ids=true | all-gather | bytes 73728 | tf_op jit(solution)/shard_map/all_gather | solution.py:80
  189.8 15.2 %all-gather.7 = f32[1,8,16,128]{2,1,0,3:T(8,128)S(1)} all-gather(f32[1,8,16,16]{2,1,0,3:T(8,128)S(1)} %copy.140), channel_id=9, replica_groups=mesh['obs'=8,'gx'=8,'gy'=4] {'obs'}, dimensions={3}, use_global_device_ids=true | all-gather | bytes 73728 | tf_op jit(solution)/shard_map/all_gather | solution.py:77
  205.8 4.4 all-to-all-start
  212.0 1.9 collective-permute-start.10
  213.9 4.1 collective-permute-start.11
  221.9 5.8 %collective-permute-start.13 = (f32[2,4,1,16,128]{4,3,2,1,0:T(8,128)S(1)}, f32[2,4,1,16,128]{4,3,2,1,0:T(8,128)S(1)}, u32[]{:S(2)}, u32[]{:S(2)}) collective-permute-start(f32[2,4,1,16,128]{4,3,2,1,0:T(8,128)S(1)} %get-tuple-element.71), channel_id=1, source_target_pairs={{0,4},{4,8},{8,12},{12,16},{16,20},{20,24},{24,28},{1,5},{5,9},{9,... | collective-permute-start | bytes 196616 | tf_op jit(solution)/shard_map/ppermute | solution.py:24
  231.6 3.9 collective-permute-start.15
  239.5 5.4 %collective-permute-start.17 = (f32[2,4,1,16,128]{4,3,2,1,0:T(8,128)S(1)}, f32[2,4,1,16,128]{4,3,2,1,0:T(8,128)S(1)}, u32[]{:S(2)}, u32[]{:S(2)}) collective-permute-start(f32[2,4,1,16,128]{4,3,2,1,0:T(8,128)S(1)} %get-tuple-element.69), channel_id=1, source_target_pairs={{0,4},{4,8},{8,12},{12,16},{16,20},{20,24},{24,28},{1,5},{5,9},{9,... | collective-permute-start | bytes 196616 | tf_op jit(solution)/shard_map/ppermute | solution.py:24
  248.8 3.9 collective-permute-start.19
  257.3 5.8 %collective-permute-start.21 = (f32[2,4,1,16,128]{4,3,2,1,0:T(8,128)S(1)}, f32[2,4,1,16,128]{4,3,2,1,0:T(8,128)S(1)}, u32[]{:S(2)}, u32[]{:S(2)}) collective-permute-start(f32[2,4,1,16,128]{4,3,2,1,0:T(8,128)S(1)} %get-tuple-element.67), channel_id=1, source_target_pairs={{0,4},{4,8},{8,12},{12,16},{16,20},{20,24},{24,28},{1,5},{5,9},{9,... | collective-permute-start | bytes 196616 | tf_op jit(solution)/shard_map/ppermute | solution.py:24
  267.0 3.9 collective-permute-start.23
  276.0 5.8 %collective-permute-start.25 = (f32[2,4,1,16,128]{4,3,2,1,0:T(8,128)}, f32[2,4,1,16,128]{4,3,2,1,0:T(8,128)S(1)}, u32[]{:S(2)}, u32[]{:S(2)}) collective-permute-start(f32[2,4,1,16,128]{4,3,2,1,0:T(8,128)} %get-tuple-element.65), channel_id=1, source_target_pairs={{0,4},{4,8},{8,12},{12,16},{16,20},{20,24},{24,28},{1,5},{5,9},{9,... | collective-permute-start | bytes 196616 | tf_op jit(solution)/shard_map/ppermute | solution.py:24
  282.5 18.6 %all-gather.6 = f32[1,8,16,128]{2,1,0,3:T(8,128)} all-gather(f32[1,8,16,16]{2,1,0,3:T(8,128)S(1)} %copy.139), channel_id=8, replica_groups=mesh['obs'=8,'gx'=8,'gy'=4] {'obs'}, dimensions={3}, use_global_device_ids=true | all-gather | bytes 73728 | tf_op jit(solution)/shard_map/all_gather | solution.py:80
  308.2 3.9 collective-permute-start.27
  316.7 5.6 %collective-permute-start.29 = (f32[2,4,1,16,128]{4,3,2,1,0:T(8,128)S(1)}, f32[2,4,1,16,128]{4,3,2,1,0:T(8,128)S(1)}, u32[]{:S(2)}, u32[]{:S(2)}) collective-permute-start(f32[2,4,1,16,128]{4,3,2,1,0:T(8,128)S(1)} %get-tuple-element.63), channel_id=1, source_target_pairs={{0,4},{4,8},{8,12},{12,16},{16,20},{20,24},{24,28},{1,5},{5,9},{9,... | collective-permute-start | bytes 196616 | tf_op jit(solution)/shard_map/ppermute | solution.py:24
  327.4 3.9 collective-permute-start.31
  335.4 5.4 %collective-permute-start.33 = (f32[2,4,1,16,128]{4,3,2,1,0:T(8,128)S(1)}, f32[2,4,1,16,128]{4,3,2,1,0:T(8,128)S(1)}, u32[]{:S(2)}, u32[]{:S(2)}) collective-permute-start(f32[2,4,1,16,128]{4,3,2,1,0:T(8,128)S(1)} %get-tuple-element.61), channel_id=1, source_target_pairs={{0,4},{4,8},{8,12},{12,16},{16,20},{20,24},{24,28},{1,5},{5,9},{9,... | collective-permute-start | bytes 196616 | tf_op jit(solution)/shard_map/ppermute | solution.py:24
  344.8 4.1 collective-permute-start.35
  348.9 4.8 collective-permute-start.53
  357.8 6.4 %collective-permute-start.37 = (f32[2,4,1,16,128]{4,3,2,1,0:T(8,128)S(1)}, f32[2,4,1,16,128]{4,3,2,1,0:T(8,128)S(1)}, u32[]{:S(2)}, u32[]{:S(2)}) collective-permute-start(f32[2,4,1,16,128]{4,3,2,1,0:T(8,128)S(1)} %get-tuple-element.59), channel_id=1, source_target_pairs={{0,4},{4,8},{8,12},{12,16},{16,20},{20,24},{24,28},{1,5},{5,9},{9,... | collective-permute-start | bytes 196616 | tf_op jit(solution)/shard_map/ppermute | solution.py:24
  368.1 3.9 collective-permute-start.39
  372.1 4.8 collective-permute-start.57
  380.9 5.8 %collective-permute-start.41 = (f32[2,4,1,16,128]{4,3,2,1,0:T(8,128)S(1)}, f32[2,4,1,16,128]{4,3,2,1,0:T(8,128)S(1)}, u32[]{:S(2)}, u32[]{:S(2)}) collective-permute-start(f32[2,4,1,16,128]{4,3,2,1,0:T(8,128)S(1)} %get-tuple-element.57), channel_id=1, source_target_pairs={{0,4},{4,8},{8,12},{12,16},{16,20},{20,24},{24,28},{1,5},{5,9},{9,... | collective-permute-start | bytes 196616 | tf_op jit(solution)/shard_map/ppermute | solution.py:24
  390.6 3.9 collective-permute-start.43
  394.5 3.9 collective-permute-start.51
  402.4 5.5 %collective-permute-start.45 = (f32[2,4,1,16,128]{4,3,2,1,0:T(8,128)S(1)}, f32[2,4,1,16,128]{4,3,2,1,0:T(8,128)S(1)}, u32[]{:S(2)}, u32[]{:S(2)}) collective-permute-start(f32[2,4,1,16,128]{4,3,2,1,0:T(8,128)S(1)} %get-tuple-element.55), channel_id=1, source_target_pairs={{0,4},{4,8},{8,12},{12,16},{16,20},{20,24},{24,28},{1,5},{5,9},{9,... | collective-permute-start | bytes 196616 | tf_op jit(solution)/shard_map/ppermute | solution.py:24
  411.7 4.1 collective-permute-start.47
  416.0 4.0 collective-permute-start.55
  420.1 2.1 collective-permute-start.58
  424.1 3.9 collective-permute-start.59
  433.6 42.0 %reduce-scatter.4.cloned.1.call-done = f32[16,128]{1,0:T(8,128)} async-done(((f32[128,128]{1,0:T(8,128)}), f32[16,128]{1,0:T(8,128)}) %reduce-scatter.4.cloned.1.call-update) | async-done | bytes 8208
  (388 shorter events, 112.5 us)
Async XLA Ops:
  8.1 92.2 %collective-permute-start.1 = (f32[2,4,1,16,128]{4,3,2,1,0:T(8,128)S(1)}, f32[2,4,1,16,128]{4,3,2,1,0:T(8,128)S(1)}, u32[]{:S(2)}, u32[]{:S(2)}) collective-permute-start(f32[2,4,1,16,128]{4,3,2,1,0:T(8,128)S(1)} %get-tuple-element.78), channel_id=1, source_target_pairs={{0,4},{4,8},{8,12},{12,16},{16,20},{20,24},{24,28},{1,5},{5,9},{9,... | collective-permute-start | bytes 196616 | tf_op jit(solution)/shard_map/ppermute | solution.py:24
  11.9 88.5 %collective-permute-start = (f32[2,4,1,16,128]{4,3,2,1,0:T(8,128)S(1)}, f32[2,4,1,16,128]{4,3,2,1,0:T(8,128)S(1)}, u32[]{:S(2)}, u32[]{:S(2)}) collective-permute-start(f32[2,4,1,16,128]{4,3,2,1,0:T(8,128)S(1)} %get-tuple-element.77), channel_id=1, source_target_pairs={{4,0},{8,4},{12,8},{16,12},{20,16},{24,20},{28,24},{5,1},{9,5},{13... | collective-permute-start | bytes 196616 | tf_op jit(solution)/shard_map/ppermute | solution.py:25
  14.2 124.2 %all-to-all-start.2 = ((f32[8,1,2048]{2,1,0:T(1,128)}), f32[8,1,2048]{2,1,0:T(1,128)S(1)}, u32[]{:S(2)}, u32[]{:S(2)}) async-start(f32[8,1,2048]{2,1,0:T(1,128)} %reshape.147), calls=%async_computation.2 | async-start | bytes 131072 | tf_op jit(solution)/shard_map/all_to_all | solution.py:13
  40.3 316.2 %collective-permute-start.48 = (f32[1,16,128]{2,1,0:T(8,128)}, f32[1,16,128]{2,1,0:T(8,128)}, u32[]{:S(2)}, u32[]{:S(2)}) collective-permute-start(f32[1,16,128]{2,1,0:T(8,128)} %get-tuple-element.98), channel_id=1, source_target_pairs={{4,0},{8,4},{12,8},{16,12},{20,16},{24,20},{28,24},{5,1},{9,5},{13... | collective-permute-start | bytes 24584 | tf_op jit(solution)/shard_map/ppermute | solution.py:25
  41.6 316.2 %collective-permute-start.49 = (f32[1,16,128]{2,1,0:T(8,128)}, f32[1,16,128]{2,1,0:T(8,128)}, u32[]{:S(2)}, u32[]{:S(2)}) collective-permute-start(f32[1,16,128]{2,1,0:T(8,128)} %get-tuple-element.97), channel_id=1, source_target_pairs={{0,4},{4,8},{8,12},{12,16},{16,20},{20,24},{24,28},{1,5},{5,9},{9,... | collective-permute-start | bytes 24584 | tf_op jit(solution)/shard_map/ppermute | solution.py:24
  63.4 316.2 %collective-permute-start.52 = (f32[1,16,128]{2,1,0:T(8,128)}, f32[1,16,128]{2,1,0:T(8,128)}, u32[]{:S(2)}, u32[]{:S(2)}) collective-permute-start(f32[1,16,128]{2,1,0:T(8,128)} %get-tuple-element.100), channel_id=1, source_target_pairs={{4,0},{8,4},{12,8},{16,12},{20,16},{24,20},{28,24},{5,1},{9,5},{13... | collective-permute-start | bytes 24584 | tf_op jit(solution)/shard_map/ppermute | solution.py:25
  100.5 37.5 %collective-permute-start.2 = (f32[2,4,10,1,128]{4,3,2,1,0:T(1,128)S(1)}, f32[2,4,10,1,128]{4,3,2,1,0:T(1,128)S(1)}, u32[]{:S(2)}, u32[]{:S(2)}) collective-permute-start(f32[2,4,10,1,128]{4,3,2,1,0:T(1,128)S(1)} %get-tuple-element.53), channel_id=1, source_target_pairs={{1,0},{2,1},{3,2},{5,4},{6,5},{7,6},{9,8},{10,9},{11,10},{13,12},{... | collective-permute-start | bytes 122888 | tf_op jit(solution)/shard_map/ppermute | solution.py:25
  103.0 35.1 %collective-permute-start.3 = (f32[2,4,10,1,128]{4,3,2,1,0:T(1,128)S(1)}, f32[2,4,10,1,128]{4,3,2,1,0:T(1,128)S(1)}, u32[]{:S(2)}, u32[]{:S(2)}) collective-permute-start(f32[2,4,10,1,128]{4,3,2,1,0:T(1,128)S(1)} %get-tuple-element.54), channel_id=1, source_target_pairs={{0,1},{1,2},{2,3},{4,5},{5,6},{6,7},{8,9},{9,10},{10,11},{12,13},{... | collective-permute-start | bytes 122888 | tf_op jit(solution)/shard_map/ppermute | solution.py:24
  138.4 67.4 %all-to-all-start.1 = ((f32[8,1,2048]{2,1,0:T(1,128)}), f32[8,1,2048]{2,1,0:T(1,128)S(1)}, u32[]{:S(2)}, u32[]{:S(2)}) async-start(f32[8,1,2048]{2,1,0:T(1,128)} %reshape.149), calls=%async_computation.1 | async-start | bytes 131072 | tf_op jit(solution)/shard_map/all_to_all | solution.py:13
  145.2 8.1 %collective-permute-start.4 = (f32[2,4,1,16,128]{4,3,2,1,0:T(8,128)S(1)}, f32[2,4,1,16,128]{4,3,2,1,0:T(8,128)S(1)}, u32[]{:S(2)}, u32[]{:S(2)}) collective-permute-start(f32[2,4,1,16,128]{4,3,2,1,0:T(8,128)S(1)} %get-tuple-element.76), channel_id=1, source_target_pairs={{4,0},{8,4},{12,8},{16,12},{20,16},{24,20},{28,24},{5,1},{9,5},{13... | collective-permute-start | bytes 196616 | tf_op jit(solution)/shard_map/ppermute | solution.py:25
  146.5 8.0 %collective-permute-start.5 = (f32[2,4,1,16,128]{4,3,2,1,0:T(8,128)S(1)}, f32[2,4,1,16,128]{4,3,2,1,0:T(8,128)S(1)}, u32[]{:S(2)}, u32[]{:S(2)}) collective-permute-start(f32[2,4,1,16,128]{4,3,2,1,0:T(8,128)S(1)} %get-tuple-element.75), channel_id=1, source_target_pairs={{0,4},{4,8},{8,12},{12,16},{16,20},{20,24},{24,28},{1,5},{5,9},{9,... | collective-permute-start | bytes 196616 | tf_op jit(solution)/shard_map/ppermute | solution.py:24
  163.5 48.4 %collective-permute-start.8 = (f32[2,4,1,16,128]{4,3,2,1,0:T(8,128)S(1)}, f32[2,4,1,16,128]{4,3,2,1,0:T(8,128)S(1)}, u32[]{:S(2)}, u32[]{:S(2)}) collective-permute-start(f32[2,4,1,16,128]{4,3,2,1,0:T(8,128)S(1)} %get-tuple-element.74), channel_id=1, source_target_pairs={{4,0},{8,4},{12,8},{16,12},{20,16},{24,20},{28,24},{5,1},{9,5},{13... | collective-permute-start | bytes 196616 | tf_op jit(solution)/shard_map/ppermute | solution.py:25
  164.8 47.1 %collective-permute-start.9 = (f32[2,4,1,16,128]{4,3,2,1,0:T(8,128)S(1)}, f32[2,4,1,16,128]{4,3,2,1,0:T(8,128)S(1)}, u32[]{:S(2)}, u32[]{:S(2)}) collective-permute-start(f32[2,4,1,16,128]{4,3,2,1,0:T(8,128)S(1)} %get-tuple-element.73), channel_id=1, source_target_pairs={{0,4},{4,8},{8,12},{12,16},{16,20},{20,24},{24,28},{1,5},{5,9},{9,... | collective-permute-start | bytes 196616 | tf_op jit(solution)/shard_map/ppermute | solution.py:24
  205.8 97.8 %all-to-all-start = ((f32[8,1,2048]{2,1,0:T(1,128)}), f32[8,1,2048]{2,1,0:T(1,128)}, u32[]{:S(2)}, u32[]{:S(2)}) async-start(f32[8,1,2048]{2,1,0:T(1,128)} %reshape.151), calls=%async_computation | async-start | bytes 131072 | tf_op jit(solution)/shard_map/all_to_all | solution.py:13
  210.2 265.5 %reduce-scatter.4.cloned.1.call-start = ((), (), s32[]{:S(2)}) async-start(), calls=%async_computation.4 | async-start | bytes 73728
  212.0 6.1 %collective-permute-start.10 = (f32[2,4,10,1,128]{4,3,2,1,0:T(1,128)S(1)}, f32[2,4,10,1,128]{4,3,2,1,0:T(1,128)S(1)}, u32[]{:S(2)}, u32[]{:S(2)}) collective-permute-start(f32[2,4,10,1,128]{4,3,2,1,0:T(1,128)S(1)} %get-tuple-element.49), channel_id=1, source_target_pairs={{1,0},{2,1},{3,2},{5,4},{6,5},{7,6},{9,8},{10,9},{11,10},{13,12},{... | collective-permute-start | bytes 122888 | tf_op jit(solution)/shard_map/ppermute | solution.py:25
  220.5 7.9 %collective-permute-start.12 = (f32[2,4,1,16,128]{4,3,2,1,0:T(8,128)S(1)}, f32[2,4,1,16,128]{4,3,2,1,0:T(8,128)S(1)}, u32[]{:S(2)}, u32[]{:S(2)}) collective-permute-start(f32[2,4,1,16,128]{4,3,2,1,0:T(8,128)S(1)} %get-tuple-element.72), channel_id=1, source_target_pairs={{4,0},{8,4},{12,8},{16,12},{20,16},{24,20},{28,24},{5,1},{9,5},{13... | collective-permute-start | bytes 196616 | tf_op jit(solution)/shard_map/ppermute | solution.py:25
  221.9 7.7 %collective-permute-start.13 = (f32[2,4,1,16,128]{4,3,2,1,0:T(8,128)S(1)}, f32[2,4,1,16,128]{4,3,2,1,0:T(8,128)S(1)}, u32[]{:S(2)}, u32[]{:S(2)}) collective-permute-start(f32[2,4,1,16,128]{4,3,2,1,0:T(8,128)S(1)} %get-tuple-element.71), channel_id=1, source_target_pairs={{0,4},{4,8},{8,12},{12,16},{16,20},{20,24},{24,28},{1,5},{5,9},{9,... | collective-permute-start | bytes 196616 | tf_op jit(solution)/shard_map/ppermute | solution.py:24
  238.2 7.1 %collective-permute-start.16 = (f32[2,4,1,16,128]{4,3,2,1,0:T(8,128)S(1)}, f32[2,4,1,16,128]{4,3,2,1,0:T(8,128)S(1)}, u32[]{:S(2)}, u32[]{:S(2)}) collective-permute-start(f32[2,4,1,16,128]{4,3,2,1,0:T(8,128)S(1)} %get-tuple-element.70), channel_id=1, source_target_pairs={{4,0},{8,4},{12,8},{16,12},{20,16},{24,20},{28,24},{5,1},{9,5},{13... | collective-permute-start | bytes 196616 | tf_op jit(solution)/shard_map/ppermute | solution.py:25
  239.5 7.3 %collective-permute-start.17 = (f32[2,4,1,16,128]{4,3,2,1,0:T(8,128)S(1)}, f32[2,4,1,16,128]{4,3,2,1,0:T(8,128)S(1)}, u32[]{:S(2)}, u32[]{:S(2)}) collective-permute-start(f32[2,4,1,16,128]{4,3,2,1,0:T(8,128)S(1)} %get-tuple-element.69), channel_id=1, source_target_pairs={{0,4},{4,8},{8,12},{12,16},{16,20},{20,24},{24,28},{1,5},{5,9},{9,... | collective-permute-start | bytes 196616 | tf_op jit(solution)/shard_map/ppermute | solution.py:24
  256.0 7.8 %collective-permute-start.20 = (f32[2,4,1,16,128]{4,3,2,1,0:T(8,128)S(1)}, f32[2,4,1,16,128]{4,3,2,1,0:T(8,128)S(1)}, u32[]{:S(2)}, u32[]{:S(2)}) collective-permute-start(f32[2,4,1,16,128]{4,3,2,1,0:T(8,128)S(1)} %get-tuple-element.68), channel_id=1, source_target_pairs={{4,0},{8,4},{12,8},{16,12},{20,16},{24,20},{28,24},{5,1},{9,5},{13... | collective-permute-start | bytes 196616 | tf_op jit(solution)/shard_map/ppermute | solution.py:25
  257.3 7.7 %collective-permute-start.21 = (f32[2,4,1,16,128]{4,3,2,1,0:T(8,128)S(1)}, f32[2,4,1,16,128]{4,3,2,1,0:T(8,128)S(1)}, u32[]{:S(2)}, u32[]{:S(2)}) collective-permute-start(f32[2,4,1,16,128]{4,3,2,1,0:T(8,128)S(1)} %get-tuple-element.67), channel_id=1, source_target_pairs={{0,4},{4,8},{8,12},{12,16},{16,20},{20,24},{24,28},{1,5},{5,9},{9,... | collective-permute-start | bytes 196616 | tf_op jit(solution)/shard_map/ppermute | solution.py:24
  274.8 31.4 %collective-permute-start.24 = (f32[2,4,1,16,128]{4,3,2,1,0:T(8,128)}, f32[2,4,1,16,128]{4,3,2,1,0:T(8,128)S(1)}, u32[]{:S(2)}, u32[]{:S(2)}) collective-permute-start(f32[2,4,1,16,128]{4,3,2,1,0:T(8,128)} %get-tuple-element.66), channel_id=1, source_target_pairs={{4,0},{8,4},{12,8},{16,12},{20,16},{24,20},{28,24},{5,1},{9,5},{13... | collective-permute-start | bytes 196616 | tf_op jit(solution)/shard_map/ppermute | solution.py:25
  276.0 30.1 %collective-permute-start.25 = (f32[2,4,1,16,128]{4,3,2,1,0:T(8,128)}, f32[2,4,1,16,128]{4,3,2,1,0:T(8,128)S(1)}, u32[]{:S(2)}, u32[]{:S(2)}) collective-permute-start(f32[2,4,1,16,128]{4,3,2,1,0:T(8,128)} %get-tuple-element.65), channel_id=1, source_target_pairs={{0,4},{4,8},{8,12},{12,16},{16,20},{20,24},{24,28},{1,5},{5,9},{9,... | collective-permute-start | bytes 196616 | tf_op jit(solution)/shard_map/ppermute | solution.py:24
  315.3 10.1 %collective-permute-start.28 = (f32[2,4,1,16,128]{4,3,2,1,0:T(8,128)S(1)}, f32[2,4,1,16,128]{4,3,2,1,0:T(8,128)S(1)}, u32[]{:S(2)}, u32[]{:S(2)}) collective-permute-start(f32[2,4,1,16,128]{4,3,2,1,0:T(8,128)S(1)} %get-tuple-element.64), channel_id=1, source_target_pairs={{4,0},{8,4},{12,8},{16,12},{20,16},{24,20},{28,24},{5,1},{9,5},{13... | collective-permute-start | bytes 196616 | tf_op jit(solution)/shard_map/ppermute | solution.py:25
  316.7 8.6 %collective-permute-start.29 = (f32[2,4,1,16,128]{4,3,2,1,0:T(8,128)S(1)}, f32[2,4,1,16,128]{4,3,2,1,0:T(8,128)S(1)}, u32[]{:S(2)}, u32[]{:S(2)}) collective-permute-start(f32[2,4,1,16,128]{4,3,2,1,0:T(8,128)S(1)} %get-tuple-element.63), channel_id=1, source_target_pairs={{0,4},{4,8},{8,12},{12,16},{16,20},{20,24},{24,28},{1,5},{5,9},{9,... | collective-permute-start | bytes 196616 | tf_op jit(solution)/shard_map/ppermute | solution.py:24
  334.0 7.2 %collective-permute-start.32 = (f32[2,4,1,16,128]{4,3,2,1,0:T(8,128)S(1)}, f32[2,4,1,16,128]{4,3,2,1,0:T(8,128)S(1)}, u32[]{:S(2)}, u32[]{:S(2)}) collective-permute-start(f32[2,4,1,16,128]{4,3,2,1,0:T(8,128)S(1)} %get-tuple-element.62), channel_id=1, source_target_pairs={{4,0},{8,4},{12,8},{16,12},{20,16},{24,20},{28,24},{5,1},{9,5},{13... | collective-permute-start | bytes 196616 | tf_op jit(solution)/shard_map/ppermute | solution.py:25
  335.4 7.3 %collective-permute-start.33 = (f32[2,4,1,16,128]{4,3,2,1,0:T(8,128)S(1)}, f32[2,4,1,16,128]{4,3,2,1,0:T(8,128)S(1)}, u32[]{:S(2)}, u32[]{:S(2)}) collective-permute-start(f32[2,4,1,16,128]{4,3,2,1,0:T(8,128)S(1)} %get-tuple-element.61), channel_id=1, source_target_pairs={{0,4},{4,8},{8,12},{12,16},{16,20},{20,24},{24,28},{1,5},{5,9},{9,... | collective-permute-start | bytes 196616 | tf_op jit(solution)/shard_map/ppermute | solution.py:24
  342.8 6.1 %collective-permute-start.34 = (f32[2,4,10,1,128]{4,3,2,1,0:T(1,128)S(1)}, f32[2,4,10,1,128]{4,3,2,1,0:T(1,128)S(1)}, u32[]{:S(2)}, u32[]{:S(2)}) collective-permute-start(f32[2,4,10,1,128]{4,3,2,1,0:T(1,128)S(1)} %get-tuple-element.37), channel_id=1, source_target_pairs={{1,0},{2,1},{3,2},{5,4},{6,5},{7,6},{9,8},{10,9},{11,10},{13,12},{... | collective-permute-start | bytes 122888 | tf_op jit(solution)/shard_map/ppermute | solution.py:25
  344.8 9.0 %collective-permute-start.35 = (f32[2,4,10,1,128]{4,3,2,1,0:T(1,128)S(1)}, f32[2,4,10,1,128]{4,3,2,1,0:T(1,128)S(1)}, u32[]{:S(2)}, u32[]{:S(2)}) collective-permute-start(f32[2,4,10,1,128]{4,3,2,1,0:T(1,128)S(1)} %get-tuple-element.38), channel_id=1, source_target_pairs={{0,1},{1,2},{2,3},{4,5},{5,6},{6,7},{8,9},{9,10},{10,11},{12,13},{... | collective-permute-start | bytes 122888 | tf_op jit(solution)/shard_map/ppermute | solution.py:24
  348.9 32.0 %collective-permute-start.53 = (f32[1,16,128]{2,1,0:T(8,128)S(1)}, f32[1,16,128]{2,1,0:T(8,128)S(1)}, u32[]{:S(2)}, u32[]{:S(2)}) collective-permute-start(f32[1,16,128]{2,1,0:T(8,128)S(1)} %copy-done.73), channel_id=1, source_target_pairs={{0,4},{4,8},{8,12},{12,16},{16,20},{20,24},{24,28},{1,5},{5,9},{9,... | collective-permute-start | bytes 24584 | tf_op jit(solution)/shard_map/ppermute | solution.py:24
  353.8 47.3 %collective-permute-start.56 = (f32[1,16,128]{2,1,0:T(8,128)S(1)}, f32[1,16,128]{2,1,0:T(8,128)S(1)}, u32[]{:S(2)}, u32[]{:S(2)}) collective-permute-start(f32[1,16,128]{2,1,0:T(8,128)S(1)} %copy-done.75), channel_id=1, source_target_pairs={{4,0},{8,4},{12,8},{16,12},{20,16},{24,20},{28,24},{5,1},{9,5},{13... | collective-permute-start | bytes 24584 | tf_op jit(solution)/shard_map/ppermute | solution.py:25
  356.5 8.5 %collective-permute-start.36 = (f32[2,4,1,16,128]{4,3,2,1,0:T(8,128)S(1)}, f32[2,4,1,16,128]{4,3,2,1,0:T(8,128)S(1)}, u32[]{:S(2)}, u32[]{:S(2)}) collective-permute-start(f32[2,4,1,16,128]{4,3,2,1,0:T(8,128)S(1)} %get-tuple-element.60), channel_id=1, source_target_pairs={{4,0},{8,4},{12,8},{16,12},{20,16},{24,20},{28,24},{5,1},{9,5},{13... | collective-permute-start | bytes 196616 | tf_op jit(solution)/shard_map/ppermute | solution.py:25
  357.8 8.3 %collective-permute-start.37 = (f32[2,4,1,16,128]{4,3,2,1,0:T(8,128)S(1)}, f32[2,4,1,16,128]{4,3,2,1,0:T(8,128)S(1)}, u32[]{:S(2)}, u32[]{:S(2)}) collective-permute-start(f32[2,4,1,16,128]{4,3,2,1,0:T(8,128)S(1)} %get-tuple-element.59), channel_id=1, source_target_pairs={{0,4},{4,8},{8,12},{12,16},{16,20},{20,24},{24,28},{1,5},{5,9},{9,... | collective-permute-start | bytes 196616 | tf_op jit(solution)/shard_map/ppermute | solution.py:24
  368.1 8.8 %collective-permute-start.39 = (f32[2,4,10,1,128]{4,3,2,1,0:T(1,128)S(1)}, f32[2,4,10,1,128]{4,3,2,1,0:T(1,128)S(1)}, u32[]{:S(2)}, u32[]{:S(2)}) collective-permute-start(f32[2,4,10,1,128]{4,3,2,1,0:T(1,128)S(1)} %get-tuple-element.36), channel_id=1, source_target_pairs={{0,1},{1,2},{2,3},{4,5},{5,6},{6,7},{8,9},{9,10},{10,11},{12,13},{... | collective-permute-start | bytes 122888 | tf_op jit(solution)/shard_map/ppermute | solution.py:24
  372.1 30.2 %collective-permute-start.57 = (f32[1,16,128]{2,1,0:T(8,128)S(1)}, f32[1,16,128]{2,1,0:T(8,128)S(1)}, u32[]{:S(2)}, u32[]{:S(2)}) collective-permute-start(f32[1,16,128]{2,1,0:T(8,128)S(1)} %copy-done.74), channel_id=1, source_target_pairs={{0,4},{4,8},{8,12},{12,16},{16,20},{20,24},{24,28},{1,5},{5,9},{9,... | collective-permute-start | bytes 24584 | tf_op jit(solution)/shard_map/ppermute | solution.py:24
  377.0 47.2 %collective-permute-start.50 = (f32[10,1,128]{2,1,0:T(1,128)S(1)}, f32[10,1,128]{2,1,0:T(1,128)S(1)}, u32[]{:S(2)}, u32[]{:S(2)}) collective-permute-start(f32[10,1,128]{2,1,0:T(1,128)S(1)} %get-tuple-element.91), channel_id=1, source_target_pairs={{1,0},{2,1},{3,2},{5,4},{6,5},{7,6},{9,8},{10,9},{11,10},{13,12},{... | collective-permute-start | bytes 15368 | tf_op jit(solution)/shard_map/ppermute | solution.py:25
  379.6 7.8 %collective-permute-start.40 = (f32[2,4,1,16,128]{4,3,2,1,0:T(8,128)S(1)}, f32[2,4,1,16,128]{4,3,2,1,0:T(8,128)S(1)}, u32[]{:S(2)}, u32[]{:S(2)}) collective-permute-start(f32[2,4,1,16,128]{4,3,2,1,0:T(8,128)S(1)} %get-tuple-element.58), channel_id=1, source_target_pairs={{4,0},{8,4},{12,8},{16,12},{20,16},{24,20},{28,24},{5,1},{9,5},{13... | collective-permute-start | bytes 196616 | tf_op jit(solution)/shard_map/ppermute | solution.py:25
  380.9 7.7 %collective-permute-start.41 = (f32[2,4,1,16,128]{4,3,2,1,0:T(8,128)S(1)}, f32[2,4,1,16,128]{4,3,2,1,0:T(8,128)S(1)}, u32[]{:S(2)}, u32[]{:S(2)}) collective-permute-start(f32[2,4,1,16,128]{4,3,2,1,0:T(8,128)S(1)} %get-tuple-element.57), channel_id=1, source_target_pairs={{0,4},{4,8},{8,12},{12,16},{16,20},{20,24},{24,28},{1,5},{5,9},{9,... | collective-permute-start | bytes 196616 | tf_op jit(solution)/shard_map/ppermute | solution.py:24
  390.6 7.9 %collective-permute-start.43 = (f32[2,4,10,1,128]{4,3,2,1,0:T(1,128)S(1)}, f32[2,4,10,1,128]{4,3,2,1,0:T(1,128)S(1)}, u32[]{:S(2)}, u32[]{:S(2)}) collective-permute-start(f32[2,4,10,1,128]{4,3,2,1,0:T(1,128)S(1)} %get-tuple-element.34), channel_id=1, source_target_pairs={{0,1},{1,2},{2,3},{4,5},{5,6},{6,7},{8,9},{9,10},{10,11},{12,13},{... | collective-permute-start | bytes 122888 | tf_op jit(solution)/shard_map/ppermute | solution.py:24
  394.5 33.6 %collective-permute-start.51 = (f32[10,1,128]{2,1,0:T(1,128)S(1)}, f32[10,1,128]{2,1,0:T(1,128)S(1)}, u32[]{:S(2)}, u32[]{:S(2)}) collective-permute-start(f32[10,1,128]{2,1,0:T(1,128)S(1)} %get-tuple-element.92), channel_id=1, source_target_pairs={{0,1},{1,2},{2,3},{4,5},{5,6},{6,7},{8,9},{9,10},{10,11},{12,13},{... | collective-permute-start | bytes 15368 | tf_op jit(solution)/shard_map/ppermute | solution.py:24
  398.5 29.7 %collective-permute-start.54 = (f32[10,1,128]{2,1,0:T(1,128)S(1)}, f32[10,1,128]{2,1,0:T(1,128)S(1)}, u32[]{:S(2)}, u32[]{:S(2)}) collective-permute-start(f32[10,1,128]{2,1,0:T(1,128)S(1)} %get-tuple-element.93), channel_id=1, source_target_pairs={{1,0},{2,1},{3,2},{5,4},{6,5},{7,6},{9,8},{10,9},{11,10},{13,12},{... | collective-permute-start | bytes 15368 | tf_op jit(solution)/shard_map/ppermute | solution.py:25
  401.1 7.1 %collective-permute-start.44 = (f32[2,4,1,16,128]{4,3,2,1,0:T(8,128)S(1)}, f32[2,4,1,16,128]{4,3,2,1,0:T(8,128)S(1)}, u32[]{:S(2)}, u32[]{:S(2)}) collective-permute-start(f32[2,4,1,16,128]{4,3,2,1,0:T(8,128)S(1)} %get-tuple-element.56), channel_id=1, source_target_pairs={{4,0},{8,4},{12,8},{16,12},{20,16},{24,20},{28,24},{5,1},{9,5},{13... | collective-permute-start | bytes 196616 | tf_op jit(solution)/shard_map/ppermute | solution.py:25
  402.4 7.4 %collective-permute-start.45 = (f32[2,4,1,16,128]{4,3,2,1,0:T(8,128)S(1)}, f32[2,4,1,16,128]{4,3,2,1,0:T(8,128)S(1)}, u32[]{:S(2)}, u32[]{:S(2)}) collective-permute-start(f32[2,4,1,16,128]{4,3,2,1,0:T(8,128)S(1)} %get-tuple-element.55), channel_id=1, source_target_pairs={{0,4},{4,8},{8,12},{12,16},{16,20},{20,24},{24,28},{1,5},{5,9},{9,... | collective-permute-start | bytes 196616 | tf_op jit(solution)/shard_map/ppermute | solution.py:24
  409.8 6.2 %collective-permute-start.46 = (f32[2,4,10,1,128]{4,3,2,1,0:T(1,128)S(1)}, f32[2,4,10,1,128]{4,3,2,1,0:T(1,128)S(1)}, u32[]{:S(2)}, u32[]{:S(2)}) collective-permute-start(f32[2,4,10,1,128]{4,3,2,1,0:T(1,128)S(1)} %get-tuple-element.31), channel_id=1, source_target_pairs={{1,0},{2,1},{3,2},{5,4},{6,5},{7,6},{9,8},{10,9},{11,10},{13,12},{... | collective-permute-start | bytes 122888 | tf_op jit(solution)/shard_map/ppermute | solution.py:25
  411.7 8.3 %collective-permute-start.47 = (f32[2,4,10,1,128]{4,3,2,1,0:T(1,128)S(1)}, f32[2,4,10,1,128]{4,3,2,1,0:T(1,128)S(1)}, u32[]{:S(2)}, u32[]{:S(2)}) collective-permute-start(f32[2,4,10,1,128]{4,3,2,1,0:T(1,128)S(1)} %get-tuple-element.32), channel_id=1, source_target_pairs={{0,1},{1,2},{2,3},{4,5},{5,6},{6,7},{8,9},{9,10},{10,11},{12,13},{... | collective-permute-start | bytes 122888 | tf_op jit(solution)/shard_map/ppermute | solution.py:24
  416.0 12.2 %collective-permute-start.55 = (f32[10,1,128]{2,1,0:T(1,128)S(1)}, f32[10,1,128]{2,1,0:T(1,128)S(1)}, u32[]{:S(2)}, u32[]{:S(2)}) collective-permute-start(f32[10,1,128]{2,1,0:T(1,128)S(1)} %get-tuple-element.94), channel_id=1, source_target_pairs={{0,1},{1,2},{2,3},{4,5},{5,6},{6,7},{8,9},{9,10},{10,11},{12,13},{... | collective-permute-start | bytes 15368 | tf_op jit(solution)/shard_map/ppermute | solution.py:24
  420.1 8.1 %collective-permute-start.58 = (f32[10,1,128]{2,1,0:T(1,128)S(1)}, f32[10,1,128]{2,1,0:T(1,128)S(1)}, u32[]{:S(2)}, u32[]{:S(2)}) collective-permute-start(f32[10,1,128]{2,1,0:T(1,128)S(1)} %get-tuple-element.95), channel_id=1, source_target_pairs={{1,0},{2,1},{3,2},{5,4},{6,5},{7,6},{9,8},{10,9},{11,10},{13,12},{... | collective-permute-start | bytes 15368 | tf_op jit(solution)/shard_map/ppermute | solution.py:25
  (96 other events, 1195.2 us)
Sparse Core Ops, SparseCore 0:
  431.8 43.7 reduce-scatter.3
